TPU v7x, 512 devices: a whole 4x8x8 slice. The times are simulated.
512 devices in a mesh: ao: 32 (over x, z), ri: 16 (over y, core).
Axes of the slice: x: 4, y: 8, z: 8, core: 2. Of those that a mesh axis runs over, the one named last changes fastest.
Arguments:
- three_center: bfloat16 [256, 12288, 128], P('ri', 'ao'), may hold values from -0.19921875 to 0.19921875
- occ_band: bfloat16 [4096, 640], P('ao'), may hold values from -0.3125 to 0.3125
- virt_band: bfloat16 [4096, 384], P('ao'), may hold values from -0.3125 to 0.3125
- three_mask: int32 [32, 3], P('ao'), may hold values 0 or 1
- occ_mask: int32 [32, 5], P('ao'), may hold values 0 or 1
- virt_mask: int32 [32, 3], P('ao'), may hold values 0 or 1
Outputs:
- chi: float32 [256, 256], P('ri')
All inputs are finite; a program needn't handle non-finite values. No bound on the sum of `three_mask` or of `occ_mask` or of `virt_mask` on one device may be relied on, other than what follows from the above.
Results may differ from a plain program's by a relative error of at most 0.004.
Values may be sent and summed in bfloat16 or wider, within the bound.
A program may use at most 64 MiB of HBM per device.

v0:
```python
import jax
import jax.numpy as jnp
from jax import lax
from jax.sharding import PartitionSpec as P


def padded_2(value, sides, width):
    for axis, dim in sides:
        peers, length = (lax.axis_size(axis), value.shape[dim])
        up = [(i, (i + 1) % peers) for i in range(peers)]
        down = [(j, i) for i, j in up]
        last = lax.slice_in_dim(value, length - width, length, axis=dim)
        initial = lax.slice_in_dim(value, 0, width, axis=dim)
        before = lax.ppermute(last, axis, up)
        after = lax.ppermute(initial, axis, down)
        value = jnp.concatenate([before, value, after], axis=dim)
    return value


def per_device(three_center, occ_band, virt_band, three_mask, occ_mask, virt_mask):
    tile_size = occ_band.shape[0]
    local_rows = three_center.shape[0]
    live_b = (
        three_center.reshape(local_rows, 3, tile_size, tile_size)
        * three_mask[0].astype(three_center.dtype)[None, :, None, None]
    )
    live_b = live_b.reshape(local_rows, 3 * tile_size, tile_size)
    live_occ = occ_band * jnp.repeat(occ_mask[0].astype(occ_band.dtype), tile_size)[None, :]
    live_virt = virt_band * jnp.repeat(virt_mask[0].astype(virt_band.dtype), tile_size)[None, :]
    occ_rows = padded_2(live_occ, (("ao", 0),), tile_size)
    blank = jnp.zeros((tile_size, tile_size), occ_band.dtype)
    green_block = jnp.concatenate(
        [
            jnp.concatenate([occ_rows[0:tile_size, tile_size:], blank], 1),
            occ_rows[tile_size : 2 * tile_size],
            jnp.concatenate([blank, occ_rows[2 * tile_size :, : 4 * tile_size]], 1),
        ],
        0,
    )
    m_local = jnp.einsum(
        "ml,pmn->pln", green_block, live_b, preferred_element_type=jnp.float32
    ).astype(jnp.bfloat16)
    padded = padded_2(m_local, (("ao", 2),), tile_size)
    needed = jnp.concatenate(
        [
            padded[:, 2 * tile_size : 5 * tile_size, 0:tile_size],
            padded[:, tile_size : 4 * tile_size, tile_size : 2 * tile_size],
            padded[:, 0 : 3 * tile_size, 2 * tile_size : 3 * tile_size],
        ],
        2,
    )
    product = jnp.einsum(
        "plv,sv->pls", needed, live_virt, preferred_element_type=jnp.float32
    ).astype(jnp.bfloat16)
    product_flat = product.reshape(local_rows, 3 * tile_size * tile_size)
    b_flat = live_b.reshape(local_rows, 3 * tile_size * tile_size)
    product_all, b_all = (
        lax.all_to_all(product_flat, "ri", split_axis=1, concat_axis=0, tiled=True),
        lax.all_to_all(b_flat, "ri", split_axis=1, concat_axis=0, tiled=True),
    )
    partial_chi = lax.dot_general(
        product_all, b_all, (((1,), (1,)), ((), ())), preferred_element_type=jnp.float32
    )
    row_panel = lax.psum_scatter(partial_chi, "ri", scatter_dimension=0, tiled=True)
    summed = lax.psum(row_panel, "ao")
    return -summed


def solution(mesh):
    placed = (
        P("ri", "ao", None),
        P("ao", None),
        P("ao", None),
        P("ao", None),
        P("ao", None),
        P("ao", None),
    )
    return jax.shard_map(
        per_device, mesh=mesh, in_specs=placed, out_specs=P("ri", None), check_vma=False
    )
```

profile of v0, /device:TPU:32, one launch (start us, length us, event | category | flops | bytes accessed | tf_op | source)
XLA Modules:
  0.0 353.9 jit_solution(3540133267525671056)
XLA Ops:
  6.5 0.7 convert_bitcast_fusion.2
  7.2 0.1 broadcast_bitcast_fusion
  7.3 0.9 broadcast_multiply_fusion.1
  8.2 4.3 %collective-permute-start = (bf16[128,640]{1,0:T(8,128)(2,1)S(1)}, bf16[128,640]{1,0:T(8,128)(2,1)}, u32[]{:S(2)}, u32[]{:S(2)}) collective-permute-start(bf16[128,640]{1,0:T(8,128)(2,1)S(1)} %broadcast_multiply_fusion.1), channel_id=1, source_target_pairs={{0,16},{16,32},{32,48},{48,64},{64,80},{80,96},{96,112},{112,128},... | collective-permute-start | bytes 491528 | tf_op jit(solution)/shard_map/ppermute | solution.py:14
  12.5 10.8 %collective-permute-start.1 = (bf16[128,640]{1,0:T(8,128)(2,1)S(1)}, bf16[128,640]{1,0:T(8,128)(2,1)}, u32[]{:S(2)}, u32[]{:S(2)}) collective-permute-start(bf16[128,640]{1,0:T(8,128)(2,1)S(1)} %broadcast_multiply_fusion.1), channel_id=1, source_target_pairs={{16,0},{32,16},{48,32},{64,48},{80,64},{96,80},{112,96},{128,112},... | collective-permute-start | bytes 491528 | tf_op jit(solution)/shard_map/ppermute | solution.py:15
  23.3 0.7 convert_bitcast_fusion.3
  23.9 0.1 mul.53
  24.1 0.0 copy-start
  24.1 2.7 reshape.31
  26.8 0.1 broadcast_bitcast_fusion.2
  26.9 0.0 collective-permute-done
  26.9 0.9 slice.20
  27.8 0.0 collective-permute-done.1
  27.8 0.9 slice.21
  28.7 0.0 copy-done
  28.7 3.3 convert_bitcast_fusion
  32.0 1.9 collective-permute-start.2
  34.0 7.2 %collective-permute-start.3 = (bf16[16,640,128]{1,2,0:T(8,128)(2,1)}, bf16[16,640,128]{1,2,0:T(8,128)(2,1)}, u32[]{:S(2)}, u32[]{:S(2)}) collective-permute-start(bf16[16,640,128]{1,2,0:T(8,128)(2,1)} %convert_bitcast_fusion), channel_id=1, source_target_pairs={{16,0},{32,16},{48,32},{64,48},{80,64},{96,80},{112,96},{128,112},... | collective-permute-start | bytes 7864328 | tf_op jit(solution)/shard_map/ppermute | solution.py:15
  41.2 0.1 broadcast_multiply_fusion
  41.3 2.0 copy.19
  43.4 0.0 copy-start.2
  43.4 7.4 %all-to-all-start.1 = ((bf16[16,16,3072]{2,0,1:T(8,128)(2,1)}), bf16[16,16,3072]{2,0,1:T(8,128)(2,1)}, u32[]{:S(2)}, u32[]{:S(2)}) async-start(bf16[16,16,3072]{2,0,1:T(8,128)(2,1)} %copy.19), calls=%async_computation.1 | async-start | bytes 3145728 | tf_op jit(solution)/shard_map/all_to_all | solution.py:59
  50.7 0.0 reduce-scatter.2.cloned.1.call-start
  50.8 0.0 copy-done.2
  50.8 0.1 broadcast_bitcast_fusion.1
  50.9 1.6 slice.23
  52.5 43.4 %collective-permute-done.2 = bf16[16,640,128]{1,2,0:T(8,128)(2,1)} collective-permute-done((bf16[16,640,128]{1,2,0:T(8,128)(2,1)}, bf16[16,640,128]{1,2,0:T(8,128)(2,1)}, u32[]{:S(2)}, u32[]{:S(2)}) %collective-permute-start.2) | collective-permute-done | bytes 2621472 | tf_op jit(solution)/shard_map/ppermute | solution.py:14
  95.9 1.6 slice.22
  97.5 0.0 copy-start.1
  97.5 0.0 collective-permute-done.3
  97.5 1.6 slice.24
  99.1 0.0 copy-done.1
  99.2 1.7 fusion.6
  100.8 0.7 all_to_all.26
  101.5 0.9 copy.18
  102.4 0.0 all-to-all-done.1
  102.4 42.5 %all_to_all.35 = bf16[16,16,3072]{2,0,1:T(8,128)(2,1)S(1)} all-to-all(bf16[16,16,3072]{2,0,1:T(8,128)(2,1)S(1)} %copy.18), channel_id=1, replica_groups=mesh['ao'=32,'ri'=16] {'ri'}, dimensions={1} | all-to-all | bytes 3145728 | tf_op jit(solution)/shard_map/all_to_all | solution.py:58
  144.9 2.7 fusion.32
  147.6 0.0 reduce-scatter.2.cloned.1.call-update
  147.6 55.1 %reduce-scatter.2.cloned.1.call-done = f32[16,256]{1,0:T(8,128)} async-done(((f32[256,256]{1,0:T(8,128)}), f32[16,256]{1,0:T(8,128)}) %reduce-scatter.2.cloned.1.call-update) | async-done | bytes 16400 | tf_op jit(solution)/shard_map/reduce_scatter | solution.py:64
  202.8 143.7 %psum.7 = f32[16,256]{1,0:T(8,128)S(1)} all-reduce(f32[16,256]{1,0:T(8,128)} %reduce-scatter.2.cloned.1.call-done), channel_id=1, replica_groups=mesh['ao'=32,'ri'=16] {'ao'}, use_global_device_ids=true, to_apply=%region_1.0 | all-reduce | flops 4096 | bytes 32768 | tf_op jit(solution)/shard_map/psum | solution.py:65
  346.5 0.6 neg.3
  (2 shorter events, 0.1 us)
Async XLA Ops:
  8.2 18.7 %collective-permute-start = (bf16[128,640]{1,0:T(8,128)(2,1)S(1)}, bf16[128,640]{1,0:T(8,128)(2,1)}, u32[]{:S(2)}, u32[]{:S(2)}) collective-permute-start(bf16[128,640]{1,0:T(8,128)(2,1)S(1)} %broadcast_multiply_fusion.1), channel_id=1, source_target_pairs={{0,16},{16,32},{32,48},{48,64},{64,80},{80,96},{96,112},{112,128},... | collective-permute-start | bytes 491528 | tf_op jit(solution)/shard_map/ppermute | solution.py:14
  12.5 15.3 %collective-permute-start.1 = (bf16[128,640]{1,0:T(8,128)(2,1)S(1)}, bf16[128,640]{1,0:T(8,128)(2,1)}, u32[]{:S(2)}, u32[]{:S(2)}) collective-permute-start(bf16[128,640]{1,0:T(8,128)(2,1)S(1)} %broadcast_multiply_fusion.1), channel_id=1, source_target_pairs={{16,0},{32,16},{48,32},{64,48},{80,64},{96,80},{112,96},{128,112},... | collective-permute-start | bytes 491528 | tf_op jit(solution)/shard_map/ppermute | solution.py:15
  24.1 4.6 %copy-start = (bf16[16,384,128]{2,1,0:T(8,128)(2,1)S(1)}, bf16[16,384,128]{2,1,0:T(8,128)(2,1)}, u32[]{:S(2)}) copy-start(bf16[16,384,128]{2,1,0:T(8,128)(2,1)} %param.6) | copy-start | bytes 4718596
  32.0 63.8 %collective-permute-start.2 = (bf16[16,640,128]{1,2,0:T(8,128)(2,1)}, bf16[16,640,128]{1,2,0:T(8,128)(2,1)}, u32[]{:S(2)}, u32[]{:S(2)}) collective-permute-start(bf16[16,640,128]{1,2,0:T(8,128)(2,1)} %convert_bitcast_fusion), channel_id=1, source_target_pairs={{0,16},{16,32},{32,48},{48,64},{64,80},{80,96},{96,112},{112,128},... | collective-permute-start | bytes 7864328 | tf_op jit(solution)/shard_map/ppermute | solution.py:14
  34.0 63.5 %collective-permute-start.3 = (bf16[16,640,128]{1,2,0:T(8,128)(2,1)}, bf16[16,640,128]{1,2,0:T(8,128)(2,1)}, u32[]{:S(2)}, u32[]{:S(2)}) collective-permute-start(bf16[16,640,128]{1,2,0:T(8,128)(2,1)} %convert_bitcast_fusion), channel_id=1, source_target_pairs={{16,0},{32,16},{48,32},{64,48},{80,64},{96,80},{112,96},{128,112},... | collective-permute-start | bytes 7864328 | tf_op jit(solution)/shard_map/ppermute | solution.py:15
  43.4 7.4 %copy-start.2 = (s32[1,3]{1,0:T(1,128)S(1)}, s32[1,3]{1,0:T(1,128)}, u32[]{:S(2)}) copy-start(s32[1,3]{1,0:T(1,128)} %param.11) | copy-start | bytes 40
  43.4 59.0 %all-to-all-start.1 = ((bf16[16,16,3072]{2,0,1:T(8,128)(2,1)}), bf16[16,16,3072]{2,0,1:T(8,128)(2,1)}, u32[]{:S(2)}, u32[]{:S(2)}) async-start(bf16[16,16,3072]{2,0,1:T(8,128)(2,1)} %copy.19), calls=%async_computation.1 | async-start | bytes 3145728 | tf_op jit(solution)/shard_map/all_to_all | solution.py:59
  50.7 152.0 %reduce-scatter.2.cloned.1.call-start = ((), (), s32[]{:S(2)}) async-start(), calls=%async_computation.3 | async-start | bytes 278528 | tf_op jit(solution)/shard_map/reduce_scatter | solution.py:64
  97.5 1.7 copy-start.1
Sparse Core Ops, SparseCore 0:
  147.8 54.9 reduce-scatter.1
where the time goes:
time: 354 us
  blocking collectives  186 us (53%)
  waiting for transfers between devices  98.6 us (28%)
  starting transfers between devices  31.6 us (9%)
  between operations  13.6 us (4%)
  local copies, waits for them, and re-layouts  13.3 us (4%)
  matrix products  7.72 us (2%)
    psum x1, blocking collectives, per_device(): summed = lax.psum(row_panel, 'ao')  144 us
    reduce_scatter x1, waiting for transfers between devices, per_device(): lax.psum_scatter(partial_chi, 'ri', scatter_dimension=0, tiled=True)  55.1 us
    ppermute x2, waiting for transfers between devices, padded_2(): before = lax.ppermute(last, axis, up)  43.4 us
    all_to_all x1, blocking collectives, per_device(): lax.all_to_all(product_flat, 'ri', split_axis=1, concat_axis=0, tiled=True)  42.5 us
    ppermute x2, starting transfers between devices, padded_2(): after = lax.ppermute(initial, axis, down)  18 us
    all_to_all x1, starting transfers between devices, per_device(): lax.all_to_all(b_flat, 'ri', split_axis=1, concat_axis=0, tiled=True)  7.36 us
  transfers between devices with their start and end apart: 6, of which 2 were waited for; matrix products, arithmetic and copies ran while one was open for 4% of the time, Pallas kernels for 0%

commit v1 on v0

--- a/solution.py
+++ b/solution.py
@@ -62,7 +62,8 @@
         product_all, b_all, (((1,), (1,)), ((), ())), preferred_element_type=jnp.float32
     )
     row_panel = lax.psum_scatter(partial_chi, "ri", scatter_dimension=0, tiled=True)
-    summed = lax.psum(row_panel, "ao")
+    shards = lax.all_gather(row_panel, "ao", axis=0, tiled=False)
+    summed = shards.sum(axis=0)
     return -summed
 
 

time: 354 us -> 264 us (0.75)
  the two profiles are of different devices: /device:TPU:32 before, /device:TPU:2 now
where the time goes in v1:
time: 264 us; the launch traced here: 263 us
  waiting for transfers between devices  102 us (39%)
  blocking collectives  95.6 us (36%)
  starting transfers between devices  28.2 us (11%)
  between operations  13.6 us (5%)
  local copies, waits for them, and re-layouts  13.3 us (5%)
  matrix products  7.72 us (3%)
  other arithmetic  3.03 us (1%)
    reduce_scatter x1, waiting for transfers between devices, per_device(): lax.psum_scatter(partial_chi, 'ri', scatter_dimension=0, tiled=True)  58.4 us
    all_gather x1, blocking collectives, per_device(): shards = lax.all_gather(row_panel, 'ao', axis=0, tiled=False)  50.2 us
    all_to_all x1, blocking collectives, per_device(): lax.all_to_all(product_flat, 'ri', split_axis=1, concat_axis=0, tiled=True)  45.4 us
    ppermute x2, waiting for transfers between devices, padded_2(): before = lax.ppermute(last, axis, up)  43.4 us
    ppermute x2, starting transfers between devices, padded_2(): after = lax.ppermute(initial, axis, down)  14.6 us
    all_to_all x1, starting transfers between devices, per_device(): lax.all_to_all(b_flat, 'ri', split_axis=1, concat_axis=0, tiled=True)  7.38 us
    ppermute x2, starting transfers between devices, padded_2(): before = lax.ppermute(last, axis, up)  6.19 us
  transfers between devices with their start and end apart: 6, of which 2 were waited for; matrix products, arithmetic and copies ran while one was open for 5% of the time, Pallas kernels for 0%

profile of v1, /device:TPU:2, one launch (start us, length us, event | category | flops | bytes accessed | tf_op | source)
XLA Modules:
  0.0 263.3 jit_solution(7124894878028157576)
XLA Ops:
  6.5 0.7 convert_bitcast_fusion.2
  7.2 0.1 broadcast_bitcast_fusion
  7.3 0.9 broadcast_multiply_fusion.1
  8.2 4.3 %collective-permute-start = (bf16[128,640]{1,0:T(8,128)(2,1)S(1)}, bf16[128,640]{1,0:T(8,128)(2,1)}, u32[]{:S(2)}, u32[]{:S(2)}) collective-permute-start(bf16[128,640]{1,0:T(8,128)(2,1)S(1)} %broadcast_multiply_fusion.1), channel_id=1, source_target_pairs={{0,16},{16,32},{32,48},{48,64},{64,80},{80,96},{96,112},{112,128},... | collective-permute-start | bytes 491528 | tf_op jit(solution)/shard_map/ppermute | solution.py:14
  12.5 8.6 %collective-permute-start.1 = (bf16[128,640]{1,0:T(8,128)(2,1)S(1)}, bf16[128,640]{1,0:T(8,128)(2,1)}, u32[]{:S(2)}, u32[]{:S(2)}) collective-permute-start(bf16[128,640]{1,0:T(8,128)(2,1)S(1)} %broadcast_multiply_fusion.1), channel_id=1, source_target_pairs={{16,0},{32,16},{48,32},{64,48},{80,64},{96,80},{112,96},{128,112},... | collective-permute-start | bytes 491528 | tf_op jit(solution)/shard_map/ppermute | solution.py:15
  21.1 0.7 convert_bitcast_fusion.3
  21.7 0.1 mul.53
  21.9 0.0 copy-start
  21.9 2.7 %reshape.31 = bf16[16,16,3072]{2,1,0:T(8,128)(2,1)S(1)} reshape(bf16[16,384,128]{2,1,0:T(8,128)(2,1)} %param.6) | data formatting | bytes 3145728 | tf_op jit(solution)/shard_map/reshape | solution.py:24
  24.6 0.1 broadcast_bitcast_fusion.2
  24.6 0.0 collective-permute-done
  24.6 0.9 slice.20
  25.6 0.0 collective-permute-done.1
  25.6 0.9 slice.21
  26.5 0.0 copy-done
  26.5 3.3 %convert_bitcast_fusion = bf16[16,640,128]{1,2,0:T(8,128)(2,1)} fusion(bf16[16,384,128]{2,1,0:T(8,128)(2,1)S(1)} %copy-done, bf16[384]{0:T(512)(128)(2,1)S(1)} %broadcast_bitcast_fusion.2, bf16[128,512]{1,0:T(8,128)(2,1)S(1)} %slice.21, bf16[128,512]{1,0:T(8,128)(2,1)S(1)} %slice.20, bf16[128,640]{1,0:T(8,128)(2,1)S(1)} %broadcast_multiply_fusion.1), kind=kOutput, calls=%fused_computation.6 | convolution fusion | flops 1011187712 | bytes 4621056 | tf_op jit(solution)/shard_map/ml,pmn->pln/dot_general | solution.py:40
  29.8 1.9 collective-permute-start.2
  31.7 6.0 %collective-permute-start.3 = (bf16[16,640,128]{1,2,0:T(8,128)(2,1)}, bf16[16,640,128]{1,2,0:T(8,128)(2,1)}, u32[]{:S(2)}, u32[]{:S(2)}) collective-permute-start(bf16[16,640,128]{1,2,0:T(8,128)(2,1)} %convert_bitcast_fusion), channel_id=1, source_target_pairs={{16,0},{32,16},{48,32},{64,48},{80,64},{96,80},{112,96},{128,112},... | collective-permute-start | bytes 7864328 | tf_op jit(solution)/shard_map/ppermute | solution.py:15
  37.8 0.1 broadcast_multiply_fusion
  37.9 2.0 copy.19
  39.9 0.0 copy-start.2
  39.9 7.4 %all-to-all-start.1 = ((bf16[16,16,3072]{2,0,1:T(8,128)(2,1)}), bf16[16,16,3072]{2,0,1:T(8,128)(2,1)}, u32[]{:S(2)}, u32[]{:S(2)}) async-start(bf16[16,16,3072]{2,0,1:T(8,128)(2,1)} %copy.19), calls=%async_computation.1 | async-start | bytes 3145728 | tf_op jit(solution)/shard_map/all_to_all | solution.py:59
  47.3 0.0 reduce-scatter.2.cloned.1.call-start
  47.4 0.0 copy-done.2
  47.4 0.1 broadcast_bitcast_fusion.1
  47.5 1.6 slice.23
  49.1 43.4 %collective-permute-done.2 = bf16[16,640,128]{1,2,0:T(8,128)(2,1)} collective-permute-done((bf16[16,640,128]{1,2,0:T(8,128)(2,1)}, bf16[16,640,128]{1,2,0:T(8,128)(2,1)}, u32[]{:S(2)}, u32[]{:S(2)}) %collective-permute-start.2) | collective-permute-done | bytes 2621472 | tf_op jit(solution)/shard_map/ppermute | solution.py:14
  92.5 1.6 slice.22
  94.1 0.0 copy-start.1
  94.1 0.0 collective-permute-done.3
  94.1 1.6 slice.24
  95.7 0.0 copy-done.1
  95.7 1.7 fusion.6
  97.4 0.7 all_to_all.26
  98.1 0.9 copy.18
  99.0 0.0 all-to-all-done.1
  99.0 45.4 %all_to_all.35 = bf16[16,16,3072]{2,0,1:T(8,128)(2,1)S(1)} all-to-all(bf16[16,16,3072]{2,0,1:T(8,128)(2,1)S(1)} %copy.18), channel_id=1, replica_groups=mesh['ao'=32,'ri'=16] {'ri'}, dimensions={1} | all-to-all | bytes 3145728 | tf_op jit(solution)/shard_map/all_to_all | solution.py:58
  144.4 2.7 %fusion.32 = f32[256,256]{1,0:T(8,128)} fusion(bf16[256,3072]{1,0:T(8,128)(2,1)S(1)} %bitcast.29, bf16[256,3072]{1,0:T(8,128)(2,1)} %bitcast.12), kind=kOutput, calls=%fused_computation.39 | convolution fusion | flops 402653184 | bytes 3407872 | tf_op jit(solution)/shard_map/dot_general | solution.py:61
  147.1 0.0 reduce-scatter.2.cloned.1.call-update
  147.2 58.4 %reduce-scatter.2.cloned.1.call-done = f32[16,256]{1,0:T(8,128)} async-done(((f32[256,256]{1,0:T(8,128)}), f32[16,256]{1,0:T(8,128)}) %reduce-scatter.2.cloned.1.call-update) | async-done | bytes 16400 | tf_op jit(solution)/shard_map/reduce_scatter | solution.py:64
  205.6 50.2 %all-gather = f32[512,256]{1,0:T(8,128)S(1)} all-gather(f32[16,256]{1,0:T(8,128)} %reduce-scatter.2.cloned.1.call-done), channel_id=2, replica_groups=mesh['ao'=32,'ri'=16] {'ao'}, dimensions={0}, use_global_device_ids=true | all-gather | bytes 540672 | tf_op jit(solution)/shard_map/all_gather | solution.py:65
  255.9 0.6 neg.3
  (3 shorter events, 0.1 us)
Async XLA Ops:
  8.2 16.4 %collective-permute-start = (bf16[128,640]{1,0:T(8,128)(2,1)S(1)}, bf16[128,640]{1,0:T(8,128)(2,1)}, u32[]{:S(2)}, u32[]{:S(2)}) collective-permute-start(bf16[128,640]{1,0:T(8,128)(2,1)S(1)} %broadcast_multiply_fusion.1), channel_id=1, source_target_pairs={{0,16},{16,32},{32,48},{48,64},{64,80},{80,96},{96,112},{112,128},... | collective-permute-start | bytes 491528 | tf_op jit(solution)/shard_map/ppermute | solution.py:14
  12.5 13.1 %collective-permute-start.1 = (bf16[128,640]{1,0:T(8,128)(2,1)S(1)}, bf16[128,640]{1,0:T(8,128)(2,1)}, u32[]{:S(2)}, u32[]{:S(2)}) collective-permute-start(bf16[128,640]{1,0:T(8,128)(2,1)S(1)} %broadcast_multiply_fusion.1), channel_id=1, source_target_pairs={{16,0},{32,16},{48,32},{64,48},{80,64},{96,80},{112,96},{128,112},... | collective-permute-start | bytes 491528 | tf_op jit(solution)/shard_map/ppermute | solution.py:15
  21.9 4.6 %copy-start = (bf16[16,384,128]{2,1,0:T(8,128)(2,1)S(1)}, bf16[16,384,128]{2,1,0:T(8,128)(2,1)}, u32[]{:S(2)}) copy-start(bf16[16,384,128]{2,1,0:T(8,128)(2,1)} %param.6) | copy-start | bytes 4718596
  29.8 62.6 %collective-permute-start.2 = (bf16[16,640,128]{1,2,0:T(8,128)(2,1)}, bf16[16,640,128]{1,2,0:T(8,128)(2,1)}, u32[]{:S(2)}, u32[]{:S(2)}) collective-permute-start(bf16[16,640,128]{1,2,0:T(8,128)(2,1)} %convert_bitcast_fusion), channel_id=1, source_target_pairs={{0,16},{16,32},{32,48},{48,64},{64,80},{80,96},{96,112},{112,128},... | collective-permute-start | bytes 7864328 | tf_op jit(solution)/shard_map/ppermute | solution.py:14
  31.7 62.3 %collective-permute-start.3 = (bf16[16,640,128]{1,2,0:T(8,128)(2,1)}, bf16[16,640,128]{1,2,0:T(8,128)(2,1)}, u32[]{:S(2)}, u32[]{:S(2)}) collective-permute-start(bf16[16,640,128]{1,2,0:T(8,128)(2,1)} %convert_bitcast_fusion), channel_id=1, source_target_pairs={{16,0},{32,16},{48,32},{64,48},{80,64},{96,80},{112,96},{128,112},... | collective-permute-start | bytes 7864328 | tf_op jit(solution)/shard_map/ppermute | solution.py:15
  39.9 7.4 %copy-start.2 = (s32[1,3]{1,0:T(1,128)S(1)}, s32[1,3]{1,0:T(1,128)}, u32[]{:S(2)}) copy-start(s32[1,3]{1,0:T(1,128)} %param.11) | copy-start | bytes 40
  39.9 59.0 %all-to-all-start.1 = ((bf16[16,16,3072]{2,0,1:T(8,128)(2,1)}), bf16[16,16,3072]{2,0,1:T(8,128)(2,1)}, u32[]{:S(2)}, u32[]{:S(2)}) async-start(bf16[16,16,3072]{2,0,1:T(8,128)(2,1)} %copy.19), calls=%async_computation.1 | async-start | bytes 3145728 | tf_op jit(solution)/shard_map/all_to_all | solution.py:59
  47.3 158.3 %reduce-scatter.2.cloned.1.call-start = ((), (), s32[]{:S(2)}) async-start(), calls=%async_computation.3 | async-start | bytes 278528 | tf_op jit(solution)/shard_map/reduce_scatter | solution.py:64
  94.1 1.7 copy-start.1
Sparse Core Ops, SparseCore 0:
  147.3 58.2 reduce-scatter.1
